TPU v7x, 256 devices: a whole 4x4x8 slice. The times are simulated.
256 devices in a mesh: kx: 32 (over x_hi, z, core), ky: 8 (over y, x_lo).
Axes of the slice: x: 4 (x_hi: 2, x_lo: 2; x = x_hi * 2 + x_lo), y: 4, z: 8, core: 2. Of those that a mesh axis runs over, the one named last changes fastest.
Arguments:
- waves: bfloat16 [2, 32, 16, 8, 1024], P(None, 'kx', 'ky'), may hold values from -0.8984375 to 0.8984375
- screened: bfloat16 [2, 2, 1024, 1024], P(None, None, 'kx'), may hold values from -0.005859375 to 0.005859375
- coulomb: float32 [1024], replicated, may hold values from 0.001 to 0.1
- transfers: int32 [2, 2], replicated, may hold values from 0 to 31, as said below
- gmap: int32 [2, 4, 1024], replicated, may hold values from 0 to 1023, as said below
Outputs:
- direct: float32 [2, 2, 32, 16, 256], P(None, None, 'kx', 'ky')
- exchange: float32 [2, 2, 32, 16, 256], P(None, None, 'kx', 'ky')
Inputs may be any that keep to these rules, and one draw needn't show every extreme that they name: transfers[j, 0] lies in 0 to 31 and transfers[j, 1] in 0 to 15; transfers[0, 1] is 15 and transfers[1, 0] is 31. Each row gmap[j, case] holds 1024 distinct plane-wave indices of 0 to 1023, among them 0 and 1023.
All inputs are finite; a program needn't handle non-finite values.
Results may differ from a plain program's by a relative error of at most 0.0072.
Values may be sent and summed in bfloat16 or wider, within the bound.
A program may use at most 64 MiB of HBM per device.

v0:
```python
import functools

import jax
import jax.numpy as jnp
import numpy as np
from jax import lax
from jax.experimental import pallas as pl
from jax.experimental.pallas import tpu as pltpu
from jax.sharding import PartitionSpec as P

MESH = pl.DeviceIdType.MESH
OFFS = (0, -1, 1, -2, 2, -3, 3, 4)
BF = jnp.bfloat16
F32 = jnp.float32
NT = (((1,), (1,)), ((), ()))


def table():
    r = np.arange(1024)
    turns = (r[:, None] * r[None, :512]) % 1024
    angles = turns.astype(np.float32) * np.float32(2.0 * np.pi / 1024)
    both = np.concatenate([np.cos(angles), np.sin(angles)], 1)
    return jnp.asarray(both, dtype=BF)


def dot(a, b):
    return lax.dot_general(a, b, (((1,), (0,)), ((), ())), preferred_element_type=F32)


def dot_nt(a, b):
    return lax.dot_general(a, b, NT, preferred_element_type=F32)


def kernel(
    transfers, waves, scr, gmap, coulomb, tab_hbm, out,
    w, hb, tb, lhs, dens, hot, bl, ap, yb, zb, res,
    tab, gm, cl, eg, fg, xa, xb, tr,
    sem_loc, zs, zr, xds, xdr, xss, xsr, ss, sr,
    es, er, eas, ear, fs, fr, fas, far, x2s, x2r,
):
    kx = lax.axis_index("kx")
    ky = lax.axis_index("ky")
    c = kx % 2
    m = kx // 2
    h = m // 8
    z = m % 8
    y = ky // 2
    xl = ky % 2

    def dev(h_, z_, c_, y_, xl_):
        return ((h_ * 8 + z_) * 2 + c_, y_ * 2 + xl_)

    def at_m(m_, c_):
        return (m_ * 2 + c_, ky)

    up = dev(h, (z + 1) % 8, c, y, xl)
    down = dev(h, (z + 7) % 8, c, y, xl)
    cross = dev(1 - h, z, c, y, 1 - xl)
    side = dev(h, z, c, y, 1 - xl)
    sib = dev(h, z, 1 - c, y, xl)
    over = dev(1 - h, z, c, y, xl)
    y_up = dev(h, z, c, (y + 1) % 4, xl)
    y_down = dev(h, z, c, (y + 3) % 4, xl)
    ky_next, ky_prev = (ky + 1) % 8, (ky + 7) % 8
    m_next, m_prev = (m + 1) % 16, (m + 15) % 16
    ahead, behind = at_m(m_next, 1), at_m(m_prev, 1)
    first = c == 0
    second = c == 1

    own_w = pltpu.make_async_copy(scr.at[c], w.at[:, h, z, c], sem_loc.at[0])
    own_w.start()
    own_h = pltpu.make_async_copy(waves.at[:, 0], hb.at[c], sem_loc.at[1])
    own_h.start()
    get_tab = pltpu.make_async_copy(tab_hbm, tab, sem_loc.at[2])
    get_tab.start()
    get_gm = pltpu.make_async_copy(gmap, gm, sem_loc.at[3])
    get_gm.start()
    get_cl = pltpu.make_async_copy(coulomb, cl, sem_loc.at[4])
    get_cl.start()
    get_tr = pltpu.make_async_copy(transfers, tr, sem_loc.at[6])
    get_tr.start()

    barrier = pltpu.get_barrier_semaphore()

    def greet(d):
        pl.semaphore_signal(barrier, inc=1, device_id=d, device_id_type=MESH)

    for d in (up, down, cross, side, sib, (m * 2, ky_next)):
        greet(d)

    @pl.when(first)
    def _():
        for d in ((m * 2, ky_prev), (m * 2 + 1, ky_prev), over):
            greet(d)
        pl.semaphore_wait(barrier, 9)

    @pl.when(second)
    def _():
        for d in (ahead, behind, y_up, y_down):
            greet(d)
        pl.semaphore_wait(barrier, 10)

    ends = {None: [], 0: [], 1: []}

    def send(src, dst, s, r, d, who=None):
        def make():
            return pltpu.make_async_remote_copy(
                src_ref=src(), dst_ref=dst(), send_sem=s(), recv_sem=r(), device_id=d, device_id_type=MESH
            )

        make().start()
        ends[who].append(make)

    def landed(dst, r):
        pltpu.make_async_remote_copy(
            src_ref=dst, dst_ref=dst, send_sem=ss.at[0], recv_sem=r, device_id=sib, device_id_type=MESH
        ).wait_recv()

    def zb_of(k):
        return (z + OFFS[k] + 8) % 8

    def half(hh, k, cc):
        return w.at[:, hh, zb_of(k), cc]

    send(lambda: waves.at[:, 0, 1], lambda: eg.at[z, c, :, 0], lambda: eas.at[0], lambda: ear.at[c, 0], (m * 2, ky_next))

    @pl.when(first)
    def _():
        pltpu.make_async_copy(waves.at[:, 0, 0], eg.at[z, 0, :, 1], sem_loc.at[5]).start()
        send(lambda: waves.at[:, 0], lambda: fg.at[y, 1], lambda: fas.at[0], lambda: far.at[1], sib, 0)

    @pl.when(second)
    def _():
        send(lambda: waves.at[:, 0, 0], lambda: eg.at[z, 1, :, 1], lambda: eas.at[1], lambda: ear.at[1, 1], sib, 1)
        send(lambda: waves.at[:, 0], lambda: fg.at[y, 0], lambda: fas.at[0], lambda: far.at[0], ahead, 1)

    send(lambda: waves.at[:, 0], lambda: hb.at[c], lambda: ss.at[0], lambda: sr.at[0], sib)
    send(lambda: scr.at[1 - c], lambda: w.at[:, h, z, c], lambda: ss.at[2], lambda: sr.at[2], sib)

    def z_send(k, cc, n, d, k2):
        send(lambda: half(h, k, cc), lambda: half(h, k, cc), lambda: zs.at[n, cc], lambda: zr.at[k2, cc], d)

    def x_send(k):
        cc = 1 - xl
        send(lambda: half(h, k, cc), lambda: half(h, k, cc), lambda: xds.at[k], lambda: xdr.at[k], cross)

    def z_recv(k, cc):
        landed(half(h, k, cc), zr.at[k, cc])

    def side_step(k):
        landed(half(1 - h, k, xl), xdr.at[k])
        send(lambda: half(1 - h, k, xl), lambda: half(1 - h, k, xl), lambda: xss.at[k], lambda: xsr.at[k], side)

    def e_send(k, p, n, d, k2):
        send(lambda: eg.at[zb_of(k), p], lambda: eg.at[zb_of(k), p], lambda: es.at[n, p], lambda: er.at[k2, p], d, 0)

    def e_recv(k, p):
        landed(eg.at[zb_of(k), p], er.at[k, p])

    def yb_of(k):
        return (y + (0, 3, 1, 2)[k]) % 4

    def f_send(k, p, n, d, k2):
        send(lambda: fg.at[yb_of(k), p], lambda: fg.at[yb_of(k), p], lambda: fs.at[n, p], lambda: fr.at[k2, p], d, 1)

    def f_recv(k, p):
        landed(fg.at[yb_of(k), p], fr.at[k, p])

    @pl.when(first)
    def _():
        landed(eg.at[z, 0, :, 0], ear.at[0, 0])
        landed(eg.at[z, 1, :, 0], ear.at[1, 0])
        landed(eg.at[z, 1, :, 1], ear.at[1, 1])
        pltpu.make_async_copy(waves.at[:, 0, 0], eg.at[z, 0, :, 1], sem_loc.at[5]).wait()
        for p in (0, 1):
            e_send(0, p, 0, up, 1)
            e_send(0, p, 1, down, 2)

    @pl.when(second)
    def _():
        for p in (1, 0):
            landed(fg.at[y, p], far.at[p])
            f_send(0, p, 0, y_up, 1)
            f_send(0, p, 1, y_down, 2)

    own_w.wait()
    landed(w.at[:, h, z, 1 - c], sr.at[2])
    for cc in (0, 1):
        z_send(0, cc, 0, up, 1)
        z_send(0, cc, 1, down, 2)
    x_send(0)

    low = lax.broadcasted_iota(jnp.int32, (8, 1024), 0) < 4
    odd = lax.broadcasted_iota(jnp.int32, (8, 1024), 1) % 2 == 1
    sign = jnp.where(odd, F32(-1.0), F32(1.0))
    sign = jnp.concatenate([sign, sign], 0)

    def left(x, at):
        rows = [jnp.broadcast_to(x[at + i : at + i + 1], (8, 1024)) for i in range(4)]
        return jnp.where(low, rows[0], rows[1]), jnp.where(low, rows[2], rows[3])

    def right(x):
        sw = pltpu.roll(x, 4, 0)
        return jnp.where(low, x, sw), jnp.where(low, sw, x)

    def pair(t, q, lr, li, rr, ri):
        re = jnp.concatenate([lr[i] * rr + li[i] * ri for i in (0, 1)], 0)
        im = jnp.concatenate([lr[i] * ri - li[i] * rr for i in (0, 1)], 0)
        lhs[t, q * 16 : q * 16 + 16] = re.astype(BF)
        lhs[t, 64 + q * 16 : 80 + q * 16] = im.astype(BF)
        lhs[t, 128 + q * 16 : 144 + q * 16] = (re * sign).astype(BF)
        lhs[t, 192 + q * 16 : 208 + q * 16] = (im * sign).astype(BF)

    def round_half(ka, kb, na, nb, cc):
        z_recv(ka, cc)
        if na is not None and (na[1] is None or cc in na[1]):
            z_send(ka, cc, na[0], up, na[2])
        z_recv(kb, cc)
        if nb is not None and (nb[1] is None or cc in nb[1]):
            z_send(kb, cc, nb[0], down, nb[2])

    def round_x(ka, kb):
        x_send(ka)
        x_send(kb)

    def transform(t):
        for g in (0, 1):
            o = dot(lhs[t, g * 128 : g * 128 + 128], tab[...])
            cols = slice(512, 1024) if g == 0 else slice(0, 512)
            dens[t, :64, cols] = (o[:64, :512] + o[64:, 512:]).astype(BF)
            dens[t, 64:, cols] = (o[64:, :512] - o[:64, 512:]).astype(BF)

    own_h.wait()
    landed(hb.at[1 - c], sr.at[0])
    for q in range(4):
        hre = hb[q // 2, 0, q % 2].astype(F32)
        him = hb[q // 2, 1, q % 2].astype(F32)
        pair(2, q, left(hre, 0), left(him, 0), right(hre)[1], right(him)[1])
    get_tab.wait()

    @pl.when(first)
    def _():
        for p in (0, 1):
            e_recv(1, p)
            e_send(1, p, 2, up, 3)
            e_recv(2, p)
            e_send(2, p, 3, down, 4)

    @pl.when(second)
    def _():
        f_recv(1, 0)
        f_send(1, 0, 2, y_up, 3)
        f_recv(2, 1)
        f_send(2, 1, 2, y_down, 3)

    round_half(1, 2, (2, None, 3), (3, None, 4), 0)
    transform(2)

    @pl.when(first)
    def _():
        for p in (0, 1):
            e_recv(3, p)
            if p == 0:
                e_send(3, p, 4, up, 5)
            else:
                e_send(3, p, 4, up, 5)
            e_recv(4, p)
            e_send(4, p, 5, down, 6)

    round_half(1, 2, (2, None, 3), (3, None, 4), 1)
    round_x(1, 2)
    side_step(0)

    get_tr.wait()
    get_gm.wait()

    @pl.when(first)
    def _():
        for p in (0, 1):
            e_recv(5, p)
            if p == 0:
                e_send(5, p, 6, up, 7)
            e_recv(6, p)
            if p == 1:
                e_send(6, p, 6, down, 7)

    def spots_y(own_ky):
        got = []
        for pt in (0, 1):
            g = own_ky * 2 + pt + tr[1, 1]
            ky_t = (g // 2) % 8
            got.append((ky_t // 2, ky_t % 2, g % 2))
        return got

    def spots_x():
        got = []
        for p in (0, 1):
            k_t = (m * 2 + p + tr[0, 0]) % 32
            got.append((k_t // 16, (k_t // 2) % 8, k_t % 2))
        return got

    @pl.when(second)
    def _():
        f_recv(1, 1)
        f_recv(2, 0)
        f_recv(3, 0)
        f_recv(3, 1)
        for pt, (y_t, _, p_t) in enumerate(spots_y(y * 2 + 1 - xl)):
            for p in (0, 1):
                for ri in (0, 1):
                    xa[pt, p, ri] = fg[y_t, p, ri, p_t]
        send(lambda: xa, lambda: xb, lambda: x2s.at[0], lambda: x2r.at[0], side, 1)

    round_half(3, 4, (4, None, 5), (5, None, 6), 0)

    @pl.when(first)
    def _():
        for p in (0, 1):
            e_recv(7, p)
        for p, (_, z_t, p_t) in enumerate(spots_x()):
            for ri in (0, 1):
                for pt in (0, 1):
                    xa[p, ri, pt] = eg[z_t, p_t, ri, pt]
        send(lambda: xa, lambda: xb, lambda: x2s.at[0], lambda: x2r.at[0], over, 0)

    round_half(3, 4, (4, None, 5), (5, None, 6), 1)
    round_x(3, 4)
    side_step(1)
    side_step(2)

    zero = lax.broadcasted_iota(jnp.int32, (8, 1024), 0) * 0

    @pl.when(first)
    def _():
        landed(xb, x2r.at[0])
        for p, (h_t, z_t, p_t) in enumerate(spots_x()):
            near = zero + h_t == h
            for ri in (0, 1):
                for pt in (0, 1):
                    tb[p, ri, pt] = jnp.where(
                        near, eg[z_t, p_t, ri, pt].astype(F32), xb[p, ri, pt].astype(F32)
                    ).astype(BF)

    @pl.when(second)
    def _():
        landed(xb, x2r.at[0])
        for pt, (y_t, xl_t, p_t) in enumerate(spots_y(ky)):
            near = zero + xl_t == xl
            for p in (0, 1):
                for ri in (0, 1):
                    tb[p, ri, pt] = jnp.where(
                        near, fg[y_t, p, ri, p_t].astype(F32), xb[pt, p, ri].astype(F32)
                    ).astype(BF)

    for q in range(4):
        p, pt = q // 2, q % 2
        hre = hb[p, 0, pt].astype(F32)
        him = hb[p, 1, pt].astype(F32)
        tre = tb[p, 0, pt].astype(F32)
        tim = tb[p, 1, pt].astype(F32)
        (trv, trc), (tiv, tic) = right(tre), right(tim)
        pair(0, q, left(hre, 4), left(him, 4), trc, tic)
        pair(1, q, left(hre, 0), left(him, 0), trv, tiv)
        pair(3, q, left(tre, 0), left(tim, 0), trc, tic)

    transform(0)
    round_half(5, 6, (6, (0,), 7), (6, (1,), 7), 0)
    transform(1)
    round_half(5, 6, (6, (0,), 7), (6, (1,), 7), 1)
    round_x(5, 6)
    side_step(3)
    side_step(4)

    def permute(q):
        p, pt = q // 2, q % 2
        wx = jnp.where(m * 2 + p + tr[c, 0] >= 32, 1, 0)
        wy = jnp.where(ky * 2 + pt + tr[c, 1] >= 16, 2, 0)
        row = gm[c, pl.ds(wx + wy, 1), :]
        hot[...] = jnp.where(
            lax.broadcasted_iota(jnp.int32, (1024, 1024), 0) == row, F32(1.0), F32(0.0)
        ).astype(BF)
        rows = jnp.concatenate(
            [
                dens[0, q * 16 : q * 16 + 16],
                dens[0, 64 + q * 16 : 80 + q * 16],
                dens[1, q * 16 : q * 16 + 16],
                dens[1, 64 + q * 16 : 80 + q * 16],
            ],
            0,
        )
        o = dot(rows, hot[...])
        for hh in (0, 1):
            cols = slice(hh * 512, hh * 512 + 512)
            ap[hh, q * 16 : q * 16 + 16] = o[0:16, cols].astype(BF)
            ap[hh, 64 + q * 16 : 80 + q * 16] = o[16:32, cols].astype(BF)
        bl[0, q * 16 : q * 16 + 16] = o[32:48].astype(BF)
        bl[0, 64 + q * 16 : 80 + q * 16] = o[48:64].astype(BF)
        bl[1, q * 16 : q * 16 + 16] = (-o[48:64]).astype(BF)
        bl[1, 64 + q * 16 : 80 + q * 16] = o[32:48].astype(BF)

    permute(0)
    permute(1)
    for cc in (0, 1):
        z_recv(7, cc)
    x_send(7)
    side_step(5)
    side_step(6)
    permute(2)
    permute(3)
    side_step(7)
    transform(3)

    row_q = lax.broadcasted_iota(jnp.int32, (64, 128), 0) // 16
    lane = lax.broadcasted_iota(jnp.int32, (64, 128), 1)
    keep = row_q == (lane % 64) // 16
    flip = jnp.where(lane < 64, F32(1.0), F32(-1.0))

    def fold(d):
        r = d[:64] + flip * pltpu.roll(d[64:], 64, 1)
        r = jnp.where(keep, r, F32(0.0))
        return (r[0:16] + r[16:32]) + (r[32:48] + r[48:64])

    get_cl.wait()
    zb[...] = (dens[3].astype(F32) * cl[...]).astype(BF)
    res[0, 1] = fold(dot_nt(dens[2], zb[...]))

    def product(hh):
        wr = w[0, hh].reshape(512, 1024)
        wi = w[1, hh].reshape(512, 1024)
        yb[...] = (dot_nt(wr, bl[0]) + dot_nt(wi, bl[1])).astype(BF)
        return dot(ap[hh], yb[...])

    d0 = product(h)
    for k in range(8):
        landed(half(1 - h, k, 1 - xl), xsr.at[k])
    res[0, 0] = fold(d0 + product(1 - h))
    out[c] = res[0]
    send(lambda: res.at[0], lambda: out.at[c], lambda: ss.at[3], lambda: sr.at[3], sib)
    landed(out.at[1 - c], sr.at[3])
    for make in ends[None]:
        make().wait_send()

    @pl.when(first)
    def _():
        for make in ends[0]:
            make().wait_send()

    @pl.when(second)
    def _():
        for make in ends[1]:
            make().wait_send()


def local(waves, screened, coulomb, transfers, gmap):
    vmem = pl.BlockSpec(memory_space=pltpu.VMEM)
    hbm = pl.BlockSpec(memory_space=pl.ANY)
    dma = pltpu.SemaphoreType.DMA
    out = pl.pallas_call(
        kernel,
        out_shape=jax.ShapeDtypeStruct((2, 2, 16, 128), F32),
        in_specs=[hbm] * 6,
        out_specs=vmem,
        scratch_shapes=[
            pltpu.VMEM((2, 2, 8, 2, 32, 1024), BF),
            pltpu.VMEM((2, 2, 2, 8, 1024), BF),
            pltpu.VMEM((2, 2, 2, 8, 1024), BF),
            pltpu.VMEM((4, 256, 1024), BF),
            pltpu.VMEM((4, 128, 1024), BF),
            pltpu.VMEM((1024, 1024), BF),
            pltpu.VMEM((2, 128, 1024), BF),
            pltpu.VMEM((2, 128, 512), BF),
            pltpu.VMEM((512, 128), BF),
            pltpu.VMEM((128, 1024), BF),
            pltpu.VMEM((1, 2, 16, 128), F32),
            pltpu.VMEM((1024, 1024), BF),
            pltpu.VMEM((2, 4, 1024), jnp.int32),
            pltpu.VMEM((1024,), F32),
            pltpu.VMEM((8, 2, 2, 2, 8, 1024), BF),
            pltpu.VMEM((4, 2, 2, 2, 8, 1024), BF),
            pltpu.VMEM((2, 2, 2, 8, 1024), BF),
            pltpu.VMEM((2, 2, 2, 8, 1024), BF),
            pltpu.SMEM((2, 2), jnp.int32),
            dma((7,)), dma((7, 2)), dma((8, 2)), dma((8,)), dma((8,)), dma((8,)), dma((8,)),
            dma((4,)), dma((4,)),
            dma((7, 2)), dma((8, 2)), dma((2,)), dma((2, 2)), dma((3, 2)), dma((4, 2)), dma((1,)), dma((2,)),
            dma((1,)), dma((1,)),
        ],
        compiler_params=pltpu.CompilerParams(
            collective_id=0, has_side_effects=True, vmem_limit_bytes=60 * 1024 * 1024
        ),
    )(transfers, waves, screened, gmap, coulomb, table())
    r = out.reshape(2, 2, 16, 2, 2, 2, 16)
    first = lax.axis_index("kx") % 2 == 0
    r = jnp.where(first, r[:, :, :, :, 0], r[:, :, :, :, 1])
    direct = r[:, 0].reshape(2, 4, 4, 2, 2, 4, 4).transpose(0, 3, 4, 5, 1, 6, 2)
    exch = r[:, 1].transpose(0, 2, 3, 1, 4)
    return direct.reshape(2, 2, 1, 2, 256), exch.reshape(2, 2, 1, 2, 256)


def solution(mesh):
    return jax.shard_map(
        local,
        mesh=mesh,
        in_specs=(P(None, "kx", "ky", None, None), P(None, None, "kx", None), P(), P(), P()),
        out_specs=(P(None, None, "kx", "ky", None), P(None, None, "kx", "ky", None)),
        check_vma=False,
    )
```

profile of v0, /device:TPU:1, one launch (start us, length us, event | category | flops | bytes accessed | tf_op | source)
XLA Modules:
  0.0 65.2 jit_solution(12541710771345224415)
XLA Ops:
  0.6 60.7 %shard_map.77 = f32[2,2,16,128]{3,2,1,0:T(8,128)} custom-call(s32[2,2]{1,0:T(2,128)} %transfers.1, bf16[2,1,2,8,1024]{4,3,2,1,0:T(8,128)(2,1)} %waves.1, bf16[2,2,32,1024]{3,2,1,0:T(8,128)(2,1)} %scr.1, s32[2,4,1024]{2,1,0:T(4,128)} %gmap.1, f32[1024]{0:T(1024)} %coulomb.1, bf16[1024,1024]{1,0:T(8,128)(2,1)} %constant.22.clone.tab_hbm), custom_call_target="tpu_custom_call" | custom-call | tf_op jit(solution)/shard_map/pallas_call | solution.py:458
  61.3 1.1 %reshape.15 = f32[2,2,16,2,2,2,16]{6,5,4,3,2,1,0:T(2,128)S(1)} reshape(f32[2,2,16,128]{3,2,1,0:T(8,128)} %shard_map.77) | data formatting | bytes 65536 | tf_op jit(solution)/shard_map/reshape | solution.py:492
  62.4 0.1 fusion
  62.6 0.7 %reshape.17 = f32[2,2,1,2,256]{4,3,2,1,0:T(2,128)} reshape(f32[2,2,2,16,16]{4,3,2,1,0:T(8,128)S(1)} %copy.9) | data formatting | bytes 16384 | tf_op jit(solution)/shard_map/reshape | solution.py:497
  63.2 0.2 reshape_squeeze.3
  63.4 0.9 %copy.8 = f32[2,4,4,2,2,4,4]{2,6,1,5,4,3,0:T(4,128)S(1)} copy(f32[2,4,4,2,2,4,4]{6,5,4,3,2,1,0:T(4,128)S(1)} %reshape_squeeze.3) | data formatting | bytes 16384 | tf_op jit(solution)/shard_map/reshape;squeeze | solution.py:495
  64.3 0.9 %reshape.16 = f32[2,2,1,2,256]{4,3,2,1,0:T(2,128)} reshape(f32[2,2,2,4,4,4,4]{6,5,4,3,2,1,0:T(4,128)S(1)} %bitcast.11) | data formatting | bytes 16384 | tf_op jit(solution)/shard_map/reshape | solution.py:497
  (2 shorter events, 0.0 us)
where the time goes:
time: 65.3 us; the launch traced here: 65.2 us
  Pallas kernels  60.7 us (93%)
  local copies, waits for them, and re-layouts  3.78 us (6%)
  between operations  0.69 us (1%)
    pallas_call x1, Pallas kernels, local(): pl.pallas_call(kernel, out_shape=jax.ShapeDtypeStruct((2, 2, 16, 128), F3...  60.7 us
    reshape x2, local copies, waits for them, and re-layouts, local(): return (direct.reshape(2, 2, 1, 2, 256), exch.reshape(2, 2, 1, 2, 256))  1.56 us

commit v1 on v0

v1 whole, which is shorter than its diff:
```python
import functools

import jax
import jax.numpy as jnp
import numpy as np
from jax import lax
from jax.experimental import pallas as pl
from jax.experimental.pallas import tpu as pltpu
from jax.sharding import PartitionSpec as P

MESH = pl.DeviceIdType.MESH
OFFS = (0, -1, 1, -2, 2, -3, 3, 4)
BF = jnp.bfloat16
F32 = jnp.float32
NT = (((1,), (1,)), ((), ()))


def table():
    r = np.arange(1024)
    turns = (r[:, None] * r[None, :512]) % 1024
    angles = turns.astype(np.float32) * np.float32(2.0 * np.pi / 1024)
    both = np.concatenate([np.cos(angles), np.sin(angles)], 1)
    return jnp.asarray(both, dtype=BF)


def dot(a, b):
    return lax.dot_general(a, b, (((1,), (0,)), ((), ())), preferred_element_type=F32)


def dot_nt(a, b):
    return lax.dot_general(a, b, NT, preferred_element_type=F32)


def kernel(
    transfers, waves, scr, gmap, coulomb, tab_hbm, out,
    w, hb, tb, lhs, dens, hot, bl, ap, blp, app, yb, zb, res, part,
    tab, gm, cl, eg, fg, xa, xb, tr,
    sem_loc, zs, zr, ys, yr, ss, sr,
    es, er, eas, ear, fs, fr, fas, far, x2s, x2r, bs, br, ps, pr,
):
    kx = lax.axis_index("kx")
    ky = lax.axis_index("ky")
    c = kx % 2
    m = kx // 2
    h = m // 8
    z = m % 8
    y = ky // 2
    xl = ky % 2
    e = y % 2

    def dev(h_, z_, c_, ky_):
        return ((h_ * 8 + z_) * 2 + c_, ky_)

    ky_next, ky_prev = (ky + 1) % 8, (ky + 7) % 8
    m_next, m_prev = (m + 1) % 16, (m + 15) % 16
    other_ky = y * 2 + 1 - xl
    up = dev(h, (z + 1) % 8, c, ky)
    down = dev(h, (z + 7) % 8, c, ky)
    cross = dev(1 - h, z, c, other_ky)
    diag = dev(1 - h, z, 1 - c, other_ky)
    side = dev(h, z, c, other_ky)
    sib = dev(h, z, 1 - c, ky)
    over = dev(1 - h, z, c, ky)
    y_up = dev(h, z, c, (ky + 2) % 8)
    y_down = dev(h, z, c, (ky + 6) % 8)
    next_near, next_far = dev(h, z, c, ky_next), dev(1 - h, z, c, ky_next)
    prev_near, prev_far = dev(h, z, c, ky_prev), dev(1 - h, z, c, ky_prev)
    ahead, behind = (m_next * 2 + 1, ky), (m_prev * 2 + 1, ky)
    last = (jnp.where(c == 0, up[0], down[0]), ky)
    last_y = (kx, jnp.where(c == 0, y_up[1], y_down[1]))
    first = c == 0
    second = c == 1

    own_w = pltpu.make_async_copy(scr.at[c], w.at[:, z, c], sem_loc.at[0])
    own_w.start()
    own_h = pltpu.make_async_copy(waves.at[:, 0], hb.at[c], sem_loc.at[1])
    own_h.start()
    get_tab = pltpu.make_async_copy(tab_hbm, tab, sem_loc.at[2])
    get_tab.start()
    get_gm = pltpu.make_async_copy(gmap, gm, sem_loc.at[3])
    get_gm.start()
    get_cl = pltpu.make_async_copy(coulomb, cl, sem_loc.at[4])
    get_cl.start()
    get_tr = pltpu.make_async_copy(transfers, tr, sem_loc.at[6])
    get_tr.start()

    barrier = pltpu.get_barrier_semaphore()

    def greet(d):
        pl.semaphore_signal(barrier, inc=1, device_id=d, device_id_type=MESH)

    for d in (up, down, cross, diag, sib, y_up, y_down):
        greet(d)

    @pl.when(first)
    def _():
        for d in (over, next_near, next_far, prev_near, prev_far):
            greet(d)
        pl.semaphore_wait(barrier, 12)

    @pl.when(second)
    def _():
        for d in (side, ahead, behind):
            greet(d)
        pl.semaphore_wait(barrier, 10)

    ends = {None: [], 0: [], 1: []}

    def send(src, dst, s, r, d, who=None):
        def make():
            return pltpu.make_async_remote_copy(
                src_ref=src(), dst_ref=dst(), send_sem=s(), recv_sem=r(), device_id=d, device_id_type=MESH
            )

        make().start()
        ends[who].append(make)

    def landed(dst, r):
        pltpu.make_async_remote_copy(
            src_ref=dst, dst_ref=dst, send_sem=ss.at[0], recv_sem=r, device_id=sib, device_id_type=MESH
        ).wait_recv()

    def zb_of(k):
        return (z + OFFS[k] + 8) % 8

    def yb_of(k):
        return (y + (0, 3, 1, 2)[k]) % 4

    def e_send(k, p, n, d, k2):
        send(lambda: eg.at[zb_of(k), p], lambda: eg.at[zb_of(k), p], lambda: es.at[n, p], lambda: er.at[k2, p], d, 0)

    def e_recv(k, p):
        landed(eg.at[zb_of(k), p], er.at[k, p])

    def f_send(k, p, n, d, k2):
        send(lambda: fg.at[yb_of(k), p], lambda: fg.at[yb_of(k), p], lambda: fs.at[n, p], lambda: fr.at[k2, p], d, 1)

    def f_recv(k, p):
        landed(fg.at[yb_of(k), p], fr.at[k, p])

    @pl.when(first)
    def _():
        send(lambda: waves.at[:, 0], lambda: eg.at[z, 0], lambda: es.at[0, 0], lambda: er.at[1, 0], up, 0)
        send(lambda: waves.at[:, 0], lambda: eg.at[z, 0], lambda: es.at[1, 0], lambda: er.at[2, 0], down, 0)
        pltpu.make_async_copy(waves.at[:, 0], eg.at[z, 0], sem_loc.at[5]).start()
        send(lambda: waves.at[:, 0], lambda: fg.at[y, 1], lambda: fas.at[0], lambda: far.at[1], sib, 0)

    @pl.when(second)
    def _():
        send(lambda: waves.at[:, 0], lambda: eg.at[z, 1], lambda: eas.at[0], lambda: ear.at[0], sib, 1)
        send(lambda: waves.at[:, 0], lambda: fg.at[y, 0], lambda: fas.at[0], lambda: far.at[0], ahead, 1)

    send(lambda: scr.at[1 - c], lambda: w.at[:, z, c], lambda: ss.at[2], lambda: sr.at[2], sib)
    send(lambda: waves.at[:, 0], lambda: hb.at[c], lambda: ss.at[0], lambda: sr.at[0], sib)

    @pl.when(first)
    def _():
        landed(eg.at[z, 1], ear.at[0])
        e_send(0, 1, 0, up, 1)
        e_send(0, 1, 1, down, 2)

    @pl.when(second)
    def _():
        for p in (1, 0):
            landed(fg.at[y, p], far.at[p])
            f_send(0, p, 0, y_up, 1)
            f_send(0, p, 1, y_down, 2)

    def block(k, cc):
        return w.at[:, zb_of(k), cc]

    def w_send(k, n, d, k2):
        send(lambda: block(k, e), lambda: block(k, e), lambda: zs.at[n], lambda: zr.at[k2], d)

    def w_recv(k):
        landed(block(k, e), zr.at[k])
        d = last_y if k == 7 else (y_up if k % 2 == 1 else y_down)
        send(lambda: block(k, e), lambda: block(k, e), lambda: ys.at[k], lambda: yr.at[k], d)

    own_w.wait()
    landed(w.at[:, z, 1 - c], sr.at[2])
    w_send(0, 0, up, 1)
    w_send(0, 1, down, 2)

    low = lax.broadcasted_iota(jnp.int32, (8, 1024), 0) < 4
    odd = lax.broadcasted_iota(jnp.int32, (8, 1024), 1) % 2 == 1
    sign = jnp.where(odd, F32(-1.0), F32(1.0))
    sign = jnp.concatenate([sign, sign], 0)

    def left(x, at):
        rows = [jnp.broadcast_to(x[at + i : at + i + 1], (8, 1024)) for i in range(4)]
        return jnp.where(low, rows[0], rows[1]), jnp.where(low, rows[2], rows[3])

    def right(x):
        sw = pltpu.roll(x, 4, 0)
        return jnp.where(low, x, sw), jnp.where(low, sw, x)

    def pair(t, q, lr, li, rr, ri):
        re = jnp.concatenate([lr[i] * rr + li[i] * ri for i in (0, 1)], 0)
        im = jnp.concatenate([lr[i] * ri - li[i] * rr for i in (0, 1)], 0)
        lhs[t, q * 16 : q * 16 + 16] = re.astype(BF)
        lhs[t, 64 + q * 16 : 80 + q * 16] = im.astype(BF)
        lhs[t, 128 + q * 16 : 144 + q * 16] = (re * sign).astype(BF)
        lhs[t, 192 + q * 16 : 208 + q * 16] = (im * sign).astype(BF)

    def transform(t):
        for g in (0, 1):
            o = dot(lhs[t, g * 128 : g * 128 + 128], tab[...])
            cols = slice(512, 1024) if g == 0 else slice(0, 512)
            dens[t, :64, cols] = (o[:64, :512] + o[64:, 512:]).astype(BF)
            dens[t, 64:, cols] = (o[64:, :512] - o[:64, 512:]).astype(BF)

    @pl.when(first)
    def _():
        for p in (0, 1):
            e_recv(1, p)
            e_send(1, p, 2, up, 3)
            e_recv(2, p)
            e_send(2, p, 3, down, 4)

    @pl.when(second)
    def _():
        f_recv(1, 0)
        f_send(1, 0, 2, y_up, 3)
        f_recv(2, 1)
        f_send(2, 1, 2, y_down, 3)

    own_h.wait()
    landed(hb.at[1 - c], sr.at[0])
    for q in range(4):
        hre = hb[q // 2, 0, q % 2].astype(F32)
        him = hb[q // 2, 1, q % 2].astype(F32)
        pair(2, q, left(hre, 0), left(him, 0), right(hre)[1], right(him)[1])
    get_tab.wait()
    get_tr.wait()
    get_gm.wait()

    def spots_y(own_ky):
        got = []
        for pt in (0, 1):
            g = own_ky * 2 + pt + tr[1, 1]
            ky_t = (g // 2) % 8
            got.append((ky_t // 2, ky_t % 2, g % 2))
        return got

    def spots_x():
        got = []
        for p in (0, 1):
            k_t = (m * 2 + p + tr[0, 0]) % 32
            got.append((k_t // 16, (k_t // 2) % 8, k_t % 2))
        return got

    @pl.when(first)
    def _():
        for p in (0, 1):
            e_recv(3, p)
            e_send(3, p, 4, up, 5)
            e_recv(4, p)
            e_send(4, p, 5, down, 6)

    @pl.when(second)
    def _():
        f_recv(1, 1)
        f_recv(2, 0)
        f_recv(3, 0)
        f_recv(3, 1)
        for pt, (y_t, _, p_t) in enumerate(spots_y(other_ky)):
            for p in (0, 1):
                for ri in (0, 1):
                    xa[pt, p, ri] = fg[y_t, p, ri, p_t]
        send(lambda: xa, lambda: xb.at[0], lambda: x2s.at[0], lambda: x2r.at[0], side, 1)

    w_recv(1)
    w_send(1, 2, up, 3)
    w_recv(2)
    w_send(2, 3, down, 4)
    transform(2)

    @pl.when(first)
    def _():
        for p in (0, 1):
            e_recv(5, p)
            if p == 0:
                e_send(5, p, 6, up, 7)
            e_recv(6, p)
            if p == 1:
                e_send(6, p, 6, down, 7)

    w_recv(3)
    w_send(3, 4, up, 5)
    w_recv(4)
    w_send(4, 5, down, 6)

    @pl.when(first)
    def _():
        pltpu.make_async_copy(waves.at[:, 0], eg.at[z, 0], sem_loc.at[5]).wait()
        for p in (0, 1):
            e_recv(7, p)
        for p, (_, z_t, p_t) in enumerate(spots_x()):
            for ri in (0, 1):
                for pt in (0, 1):
                    xa[pt, p, ri] = eg[z_t, p_t, ri, pt]
        send(lambda: xa.at[1], lambda: xb.at[1, 0], lambda: x2s.at[1], lambda: x2r.at[1], next_near, 0)
        send(lambda: xa.at[1], lambda: xb.at[1, 1], lambda: x2s.at[2], lambda: x2r.at[2], next_far, 0)
        send(lambda: xa.at[0], lambda: xb.at[0, 0], lambda: x2s.at[0], lambda: x2r.at[0], over, 0)

    w_recv(5)
    w_recv(6)
    k_last = jnp.where(c == 0, (z + 5) % 8, (z + 3) % 8)
    send(lambda: w.at[:, k_last, e], lambda: w.at[:, k_last, e], lambda: zs.at[6], lambda: zr.at[7], last)

    zero = lax.broadcasted_iota(jnp.int32, (8, 1024), 0) * 0

    @pl.when(first)
    def _():
        landed(xb.at[0, 0], x2r.at[0])
        landed(xb.at[1, 0], x2r.at[1])
        landed(xb.at[1, 1], x2r.at[2])
        for p, (h_t, _, _) in enumerate(spots_x()):
            near = zero + h_t == h
            for ri in (0, 1):
                tb[p, ri, 1] = jnp.where(near, xa[0, p, ri].astype(F32), xb[0, 0, p, ri].astype(F32)).astype(BF)
                tb[p, ri, 0] = jnp.where(near, xb[1, 0, p, ri].astype(F32), xb[1, 1, p, ri].astype(F32)).astype(BF)

    @pl.when(second)
    def _():
        landed(xb.at[0], x2r.at[0])
        for pt, (y_t, xl_t, p_t) in enumerate(spots_y(ky)):
            near = zero + xl_t == xl
            for p in (0, 1):
                for ri in (0, 1):
                    tb[p, ri, pt] = jnp.where(
                        near, fg[y_t, p, ri, p_t].astype(F32), xb[0, pt, p, ri].astype(F32)
                    ).astype(BF)

    for q in range(4):
        p, pt = q // 2, q % 2
        hre = hb[p, 0, pt].astype(F32)
        him = hb[p, 1, pt].astype(F32)
        tre = tb[p, 0, pt].astype(F32)
        tim = tb[p, 1, pt].astype(F32)
        (trv, trc), (tiv, tic) = right(tre), right(tim)
        pair(0, q, left(hre, 4), left(him, 4), trc, tic)
        pair(1, q, left(hre, 0), left(him, 0), trv, tiv)
        pair(3, q, left(tre, 0), left(tim, 0), trc, tic)

    transform(0)
    transform(1)

    def permute(q):
        p, pt = q // 2, q % 2
        wx = jnp.where(m * 2 + p + tr[c, 0] >= 32, 1, 0)
        wy = jnp.where(ky * 2 + pt + tr[c, 1] >= 16, 2, 0)
        row = gm[c, pl.ds(wx + wy, 1), :]
        hot[...] = jnp.where(
            lax.broadcasted_iota(jnp.int32, (1024, 1024), 0) == row, F32(1.0), F32(0.0)
        ).astype(BF)
        at = slice(q * 16, q * 16 + 16)
        rows = jnp.concatenate(
            [dens[0, at], dens[0, 64 + q * 16 : 80 + q * 16], dens[1, at], dens[1, 64 + q * 16 : 80 + q * 16]], 0
        )
        o = dot(rows, hot[...]).astype(BF)
        for hh in (0, 1):
            cols = slice(hh * 512, hh * 512 + 512)
            ap[hh, 0, at] = o[0:16, cols]
            ap[hh, 1, at] = o[16:32, cols]
        bl[0, 0, at] = o[32:48]
        bl[0, 1, at] = o[48:64]
        bl[1, 0, at] = -o[48:64]
        bl[1, 1, at] = o[32:48]

    def share(p):
        at = pl.ds(p * 32, 32)
        send(lambda: bl.at[0, :, at], lambda: blp.at[0, :, at], lambda: bs.at[p, 0], lambda: br.at[p, 0], cross)
        send(lambda: ap.at[1 - h, :, at], lambda: app.at[:, at], lambda: bs.at[p, 1], lambda: br.at[p, 1], cross)

    permute(0)
    permute(1)
    share(0)
    w_recv(7)
    permute(2)
    permute(3)
    share(1)

    row_q = lax.broadcasted_iota(jnp.int32, (64, 128), 0) // 16
    lane = lax.broadcasted_iota(jnp.int32, (64, 128), 1)
    keep = row_q == (lane % 64) // 16
    flip = jnp.where(lane < 64, F32(1.0), F32(-1.0))

    def fold(d):
        r = d[:64] + flip * pltpu.roll(d[64:], 64, 1)
        r = jnp.where(keep, r, F32(0.0))
        return (r[0:16] + r[16:32]) + (r[32:48] + r[48:64])

    transform(3)
    get_cl.wait()
    zb[...] = (dens[3].astype(F32) * cl[...]).astype(BF)
    res[1] = fold(dot_nt(dens[2], zb[...]))

    for k in range(1, 8):
        landed(block(k, 1 - e), yr.at[k])

    def product(b, a):
        wr = w[0].reshape(512, 1024)
        wi = w[1].reshape(512, 1024)
        yb[...] = (dot_nt(wr, b[0].reshape(128, 1024)) + dot_nt(wi, b[1].reshape(128, 1024))).astype(BF)
        return fold(dot(a.reshape(128, 512), yb[...]))

    res[0] = product(bl, ap[h])
    for p in (0, 1):
        at = pl.ds(p * 32, 32)
        landed(blp.at[0, :, at], br.at[p, 0])
        landed(app.at[:, at], br.at[p, 1])
    blp[1, 0] = -blp[0, 1]
    blp[1, 1] = blp[0, 0]
    send(lambda: res, lambda: part.at[0], lambda: ps.at[0], lambda: pr.at[0], sib)
    res_far = product(blp, app[...])
    part[3, 0] = res_far
    send(lambda: part.at[3, 0], lambda: part.at[1, 0], lambda: ps.at[1], lambda: pr.at[1], cross)
    send(lambda: part.at[3, 0], lambda: part.at[2, 0], lambda: ps.at[2], lambda: pr.at[2], diag)
    landed(part.at[0], pr.at[0])
    landed(part.at[1, 0], pr.at[1])
    landed(part.at[2, 0], pr.at[2])
    out[c, 0] = res[0] + part[1, 0]
    out[c, 1] = res[1]
    out[1 - c, 0] = part[0, 0] + part[2, 0]
    out[1 - c, 1] = part[0, 1]
    for make in ends[None]:
        make().wait_send()

    @pl.when(first)
    def _():
        for make in ends[0]:
            make().wait_send()

    @pl.when(second)
    def _():
        for make in ends[1]:
            make().wait_send()


def local(waves, screened, coulomb, transfers, gmap):
    vmem = pl.BlockSpec(memory_space=pltpu.VMEM)
    hbm = pl.BlockSpec(memory_space=pl.ANY)
    dma = pltpu.SemaphoreType.DMA
    out = pl.pallas_call(
        kernel,
        out_shape=jax.ShapeDtypeStruct((2, 2, 16, 128), F32),
        in_specs=[hbm] * 6,
        out_specs=vmem,
        scratch_shapes=[
            pltpu.VMEM((2, 8, 2, 32, 1024), BF),
            pltpu.VMEM((2, 2, 2, 8, 1024), BF),
            pltpu.VMEM((2, 2, 2, 8, 1024), BF),
            pltpu.VMEM((4, 256, 1024), BF),
            pltpu.VMEM((4, 128, 1024), BF),
            pltpu.VMEM((1024, 1024), BF),
            pltpu.VMEM((2, 2, 64, 1024), BF),
            pltpu.VMEM((2, 2, 64, 512), BF),
            pltpu.VMEM((2, 2, 64, 1024), BF),
            pltpu.VMEM((2, 64, 512), BF),
            pltpu.VMEM((512, 128), BF),
            pltpu.VMEM((128, 1024), BF),
            pltpu.VMEM((2, 16, 128), F32),
            pltpu.VMEM((4, 2, 16, 128), F32),
            pltpu.VMEM((1024, 1024), BF),
            pltpu.VMEM((2, 4, 1024), jnp.int32),
            pltpu.VMEM((1024,), F32),
            pltpu.VMEM((8, 2, 2, 2, 8, 1024), BF),
            pltpu.VMEM((4, 2, 2, 2, 8, 1024), BF),
            pltpu.VMEM((2, 2, 2, 8, 1024), BF),
            pltpu.VMEM((2, 2, 2, 2, 8, 1024), BF),
            pltpu.SMEM((2, 2), jnp.int32),
            dma((7,)), dma((7,)), dma((8,)), dma((8,)), dma((8,)), dma((4,)), dma((4,)),
            dma((7, 2)), dma((8, 2)), dma((1,)), dma((1,)), dma((3, 2)), dma((4, 2)), dma((1,)), dma((2,)),
            dma((3,)), dma((3,)), dma((2, 2)), dma((2, 2)), dma((3,)), dma((3,)),
        ],
        compiler_params=pltpu.CompilerParams(
            collective_id=0, has_side_effects=True, vmem_limit_bytes=60 * 1024 * 1024
        ),
    )(transfers, waves, screened, gmap, coulomb, table())
    r = out.reshape(2, 2, 16, 2, 2, 2, 16)
    first = lax.axis_index("kx") % 2 == 0
    r = jnp.where(first, r[:, :, :, :, 0], r[:, :, :, :, 1])
    direct = r[:, 0].reshape(2, 4, 4, 2, 2, 4, 4).transpose(0, 3, 4, 5, 1, 6, 2)
    exch = r[:, 1].transpose(0, 2, 3, 1, 4)
    return direct.reshape(2, 2, 1, 2, 256), exch.reshape(2, 2, 1, 2, 256)


def solution(mesh):
    return jax.shard_map(
        local,
        mesh=mesh,
        in_specs=(P(None, "kx", "ky", None, None), P(None, None, "kx", None), P(), P(), P()),
        out_specs=(P(None, None, "kx", "ky", None), P(None, None, "kx", "ky", None)),
        check_vma=False,
    )
```

time: 65.3 us -> 53.7 us (0.82)
  Pallas kernels: 60.7 us -> 49 us
    pallas_call x1, Pallas kernels: 60.7 us -> 49 us  [local(): pl.pallas_call(kernel, out_shape=jax.ShapeDtypeStruct((2, 2, 16, 128), F3...]
where the time goes in v1:
time: 53.7 us; the launch traced here: 53.6 us
  Pallas kernels  49 us (91%)
  local copies, waits for them, and re-layouts  3.78 us (7%)
  between operations  0.69 us (1%)
    pallas_call x1, Pallas kernels, local(): pl.pallas_call(kernel, out_shape=jax.ShapeDtypeStruct((2, 2, 16, 128), F3...  49 us
    reshape x2, local copies, waits for them, and re-layouts, local(): return (direct.reshape(2, 2, 1, 2, 256), exch.reshape(2, 2, 1, 2, 256))  1.56 us
    reshape x1, local copies, waits for them, and re-layouts, local(): r = out.reshape(2, 2, 16, 2, 2, 2, 16)  1.13 us
    another operation x2, local copies, waits for them, and re-layouts, local(): direct = r[:, 0].reshape(2, 4, 4, 2, 2, 4, 4).transpose(0, 3, 4, 5, 1, 6, 2)  1.07 us

profile of v1, /device:TPU:1, one launch (start us, length us, event | category | flops | bytes accessed | tf_op | source)
XLA Modules:
  0.0 53.6 jit_solution(14297041797756486038)
XLA Ops:
  0.6 49.0 %shard_map.77 = f32[2,2,16,128]{3,2,1,0:T(8,128)} custom-call(s32[2,2]{1,0:T(2,128)} %transfers.1, bf16[2,1,2,8,1024]{4,3,2,1,0:T(8,128)(2,1)} %waves.1, bf16[2,2,32,1024]{3,2,1,0:T(8,128)(2,1)} %scr.1, s32[2,4,1024]{2,1,0:T(4,128)} %gmap.1, f32[1024]{0:T(1024)} %coulomb.1, bf16[1024,1024]{1,0:T(8,128)(2,1)} %constant.22.clone.tab_hbm), custom_call_target="tpu_custom_call" | custom-call | tf_op jit(solution)/shard_map/pallas_call | solution.py:446
  49.7 1.1 %reshape.15 = f32[2,2,16,2,2,2,16]{6,5,4,3,2,1,0:T(2,128)S(1)} reshape(f32[2,2,16,128]{3,2,1,0:T(8,128)} %shard_map.77) | data formatting | bytes 65536 | tf_op jit(solution)/shard_map/reshape | solution.py:482
  50.8 0.1 fusion
  50.9 0.7 %reshape.17 = f32[2,2,1,2,256]{4,3,2,1,0:T(2,128)} reshape(f32[2,2,2,16,16]{4,3,2,1,0:T(8,128)S(1)} %copy.9) | data formatting | bytes 16384 | tf_op jit(solution)/shard_map/reshape | solution.py:487
  51.6 0.2 reshape_squeeze.3
  51.8 0.9 %copy.8 = f32[2,4,4,2,2,4,4]{2,6,1,5,4,3,0:T(4,128)S(1)} copy(f32[2,4,4,2,2,4,4]{6,5,4,3,2,1,0:T(4,128)S(1)} %reshape_squeeze.3) | data formatting | bytes 16384 | tf_op jit(solution)/shard_map/reshape;squeeze | solution.py:485
  52.7 0.9 %reshape.16 = f32[2,2,1,2,256]{4,3,2,1,0:T(2,128)} reshape(f32[2,2,2,4,4,4,4]{6,5,4,3,2,1,0:T(4,128)S(1)} %bitcast.11) | data formatting | bytes 16384 | tf_op jit(solution)/shard_map/reshape | solution.py:487
  (2 shorter events, 0.0 us)

commit v2 on v1

--- a/solution.py
+++ b/solution.py
@@ -34,9 +34,9 @@
 def kernel(
     transfers, waves, scr, gmap, coulomb, tab_hbm, out,
     w, hb, tb, lhs, dens, hot, bl, ap, blp, app, yb, zb, res, part,
-    tab, gm, cl, eg, fg, xa, xb, tr,
-    sem_loc, zs, zr, ys, yr, ss, sr,
-    es, er, eas, ear, fs, fr, fas, far, x2s, x2r, bs, br, ps, pr,
+    tab, gm, cl, eg, vg, fg, xa, xb, tr,
+    sem_loc, zs, zr, qs, qr, ys, yr, ss, sr,
+    es, er, vs, vr, fs, fr, fas, far, x2s, x2r, bs, br, ps, pr,
 ):
     kx = lax.axis_index("kx")
     ky = lax.axis_index("ky")
@@ -65,6 +65,9 @@
     y_down = dev(h, z, c, (ky + 6) % 8)
     next_near, next_far = dev(h, z, c, ky_next), dev(1 - h, z, c, ky_next)
     prev_near, prev_far = dev(h, z, c, ky_prev), dev(1 - h, z, c, ky_prev)
+    far_up, far_down = (z + 3) % 8, (z + 5) % 8
+    reach = [dev(h, far_up, 0, ky), dev(h, far_down, 0, ky)]
+    reach_b = [dev(h, far_up, 1, ky), dev(h, far_down, 1, ky)]
     ahead, behind = (m_next * 2 + 1, ky), (m_prev * 2 + 1, ky)
     last = (jnp.where(c == 0, up[0], down[0]), ky)
     last_y = (kx, jnp.where(c == 0, y_up[1], y_down[1]))
@@ -89,20 +92,20 @@
     def greet(d):
         pl.semaphore_signal(barrier, inc=1, device_id=d, device_id_type=MESH)
 
-    for d in (up, down, cross, diag, sib, y_up, y_down):
+    for d in (up, down, cross, diag, side, sib, y_up, y_down, reach[0], reach[1]):
         greet(d)
 
     @pl.when(first)
     def _():
-        for d in (over, next_near, next_far, prev_near, prev_far):
+        for d in (over, next_near, next_far, prev_near, prev_far, reach_b[0], reach_b[1]):
+            greet(d)
+        pl.semaphore_wait(barrier, 17)
+
+    @pl.when(second)
+    def _():
+        for d in (ahead, behind):
             greet(d)
         pl.semaphore_wait(barrier, 12)
-
-    @pl.when(second)
-    def _():
-        for d in (side, ahead, behind):
-            greet(d)
-        pl.semaphore_wait(barrier, 10)
 
     ends = {None: [], 0: [], 1: []}
 
@@ -126,38 +129,30 @@
     def yb_of(k):
         return (y + (0, 3, 1, 2)[k]) % 4
 
-    def e_send(k, p, n, d, k2):
-        send(lambda: eg.at[zb_of(k), p], lambda: eg.at[zb_of(k), p], lambda: es.at[n, p], lambda: er.at[k2, p], d, 0)
-
-    def e_recv(k, p):
-        landed(eg.at[zb_of(k), p], er.at[k, p])
-
     def f_send(k, p, n, d, k2):
         send(lambda: fg.at[yb_of(k), p], lambda: fg.at[yb_of(k), p], lambda: fs.at[n, p], lambda: fr.at[k2, p], d, 1)
 
     def f_recv(k, p):
         landed(fg.at[yb_of(k), p], fr.at[k, p])
 
+    @pl.when(second)
+    def _():
+        send(lambda: waves.at[:, 0], lambda: fg.at[y, 0], lambda: fas.at[0], lambda: far.at[0], ahead, 1)
+
+    send(lambda: waves.at[:, 0], lambda: eg.at[0, c], lambda: es.at[0], lambda: er.at[0, c], reach[0])
+    send(lambda: waves.at[:, 0], lambda: eg.at[2, c], lambda: es.at[1], lambda: er.at[2, c], reach[1])
+
     @pl.when(first)
     def _():
-        send(lambda: waves.at[:, 0], lambda: eg.at[z, 0], lambda: es.at[0, 0], lambda: er.at[1, 0], up, 0)
-        send(lambda: waves.at[:, 0], lambda: eg.at[z, 0], lambda: es.at[1, 0], lambda: er.at[2, 0], down, 0)
-        pltpu.make_async_copy(waves.at[:, 0], eg.at[z, 0], sem_loc.at[5]).start()
+        pltpu.make_async_copy(waves.at[:, 0], eg.at[1, 0], sem_loc.at[5]).start()
         send(lambda: waves.at[:, 0], lambda: fg.at[y, 1], lambda: fas.at[0], lambda: far.at[1], sib, 0)
 
     @pl.when(second)
     def _():
-        send(lambda: waves.at[:, 0], lambda: eg.at[z, 1], lambda: eas.at[0], lambda: ear.at[0], sib, 1)
-        send(lambda: waves.at[:, 0], lambda: fg.at[y, 0], lambda: fas.at[0], lambda: far.at[0], ahead, 1)
+        send(lambda: waves.at[:, 0], lambda: eg.at[1, 1], lambda: es.at[2], lambda: er.at[1, 1], sib, 1)
 
     send(lambda: scr.at[1 - c], lambda: w.at[:, z, c], lambda: ss.at[2], lambda: sr.at[2], sib)
     send(lambda: waves.at[:, 0], lambda: hb.at[c], lambda: ss.at[0], lambda: sr.at[0], sib)
-
-    @pl.when(first)
-    def _():
-        landed(eg.at[z, 1], ear.at[0])
-        e_send(0, 1, 0, up, 1)
-        e_send(0, 1, 1, down, 2)
 
     @pl.when(second)
     def _():
@@ -166,22 +161,41 @@
             f_send(0, p, 0, y_up, 1)
             f_send(0, p, 1, y_down, 2)
 
-    def block(k, cc):
-        return w.at[:, zb_of(k), cc]
+    def block(k, cc, ri):
+        return w.at[ri, zb_of(k), cc]
+
+    def hand(src, sems, there, d):
+        send(lambda: src, lambda: src, lambda: sems, lambda: there, d)
 
     def w_send(k, n, d, k2):
-        send(lambda: block(k, e), lambda: block(k, e), lambda: zs.at[n], lambda: zr.at[k2], d)
+        hand(block(k, e, xl), zs.at[n], zr.at[k2], d)
+
+    def y_way(k):
+        return last_y if k == 7 else (y_up if k % 2 == 1 else y_down)
 
     def w_recv(k):
-        landed(block(k, e), zr.at[k])
-        d = last_y if k == 7 else (y_up if k % 2 == 1 else y_down)
-        send(lambda: block(k, e), lambda: block(k, e), lambda: ys.at[k], lambda: yr.at[k], d)
+        landed(block(k, e, xl), zr.at[k])
+
+    def w_spread(k):
+        hand(block(k, e, xl), qs.at[k], qr.at[k], side)
+        hand(block(k, e, xl), ys.at[k, 0], yr.at[k, 0], y_way(k))
+
+    def s_relay(k):
+        landed(block(k, e, 1 - xl), qr.at[k])
+        hand(block(k, e, 1 - xl), ys.at[k, 1], yr.at[k, 1], y_way(k))
 
     own_w.wait()
     landed(w.at[:, z, 1 - c], sr.at[2])
     w_send(0, 0, up, 1)
     w_send(0, 1, down, 2)
 
+    @pl.when(second)
+    def _():
+        f_recv(1, 0)
+        f_send(1, 0, 2, y_up, 3)
+        f_recv(2, 1)
+        f_send(2, 1, 2, y_down, 3)
+
     low = lax.broadcasted_iota(jnp.int32, (8, 1024), 0) < 4
     odd = lax.broadcasted_iota(jnp.int32, (8, 1024), 1) % 2 == 1
     sign = jnp.where(odd, F32(-1.0), F32(1.0))
@@ -198,10 +212,14 @@
     def pair(t, q, lr, li, rr, ri):
         re = jnp.concatenate([lr[i] * rr + li[i] * ri for i in (0, 1)], 0)
         im = jnp.concatenate([lr[i] * ri - li[i] * rr for i in (0, 1)], 0)
-        lhs[t, q * 16 : q * 16 + 16] = re.astype(BF)
-        lhs[t, 64 + q * 16 : 80 + q * 16] = im.astype(BF)
-        lhs[t, 128 + q * 16 : 144 + q * 16] = (re * sign).astype(BF)
-        lhs[t, 192 + q * 16 : 208 + q * 16] = (im * sign).astype(BF)
+        if t < 2:
+            slot, at, gap = q // 2, t * 64 + (q % 2) * 16, 32
+        else:
+            slot, at, gap = t, q * 16, 64
+        lhs[slot, at : at + 16] = re.astype(BF)
+        lhs[slot, at + gap : at + gap + 16] = im.astype(BF)
+        lhs[slot, at + 128 : at + 144] = (re * sign).astype(BF)
+        lhs[slot, at + gap + 128 : at + gap + 144] = (im * sign).astype(BF)
 
     def transform(t):
         for g in (0, 1):
@@ -209,21 +227,6 @@
             cols = slice(512, 1024) if g == 0 else slice(0, 512)
             dens[t, :64, cols] = (o[:64, :512] + o[64:, 512:]).astype(BF)
             dens[t, 64:, cols] = (o[64:, :512] - o[:64, 512:]).astype(BF)
-
-    @pl.when(first)
-    def _():
-        for p in (0, 1):
-            e_recv(1, p)
-            e_send(1, p, 2, up, 3)
-            e_recv(2, p)
-            e_send(2, p, 3, down, 4)
-
-    @pl.when(second)
-    def _():
-        f_recv(1, 0)
-        f_send(1, 0, 2, y_up, 3)
-        f_recv(2, 1)
-        f_send(2, 1, 2, y_down, 3)
 
     own_h.wait()
     landed(hb.at[1 - c], sr.at[0])
@@ -246,17 +249,33 @@
     def spots_x():
         got = []
         for p in (0, 1):
-            k_t = (m * 2 + p + tr[0, 0]) % 32
-            got.append((k_t // 16, (k_t // 2) % 8, k_t % 2))
+            step = p + tr[0, 0]
+            d = (step // 2) % 8
+            a = jnp.where(d >= 5, jnp.where(d >= 7, 0, -1), jnp.where(d >= 2, 1, 0))
+            b = (d - 3 * a + 9) % 8 - 1
+            got.append((((m * 2 + step) % 32) // 16, a + 1, b + 1, step % 2))
         return got
 
+    w_recv(1)
+    w_send(1, 2, up, 3)
+    w_recv(2)
+    w_send(2, 3, down, 4)
+    w_spread(1)
+    w_spread(2)
+
     @pl.when(first)
     def _():
-        for p in (0, 1):
-            e_recv(3, p)
-            e_send(3, p, 4, up, 5)
-            e_recv(4, p)
-            e_send(4, p, 5, down, 6)
+        pltpu.make_async_copy(waves.at[:, 0], eg.at[1, 0], sem_loc.at[5]).wait()
+        landed(eg.at[1, 1], er.at[1, 1])
+        for a in (0, 2):
+            for p in (0, 1):
+                landed(eg.at[a, p], er.at[a, p])
+        for p, (_, a, _, p_t) in enumerate(spots_x()):
+            for ri in (0, 1):
+                for pt in (0, 1):
+                    vg[1, p, ri, pt] = eg[a, p_t, ri, pt]
+        send(lambda: vg.at[1], lambda: vg.at[0], lambda: vs.at[0], lambda: vr.at[0], up, 0)
+        send(lambda: vg.at[1], lambda: vg.at[2], lambda: vs.at[1], lambda: vr.at[1], down, 0)
 
     @pl.when(second)
     def _():
@@ -270,22 +289,6 @@
                     xa[pt, p, ri] = fg[y_t, p, ri, p_t]
         send(lambda: xa, lambda: xb.at[0], lambda: x2s.at[0], lambda: x2r.at[0], side, 1)
 
-    w_recv(1)
-    w_send(1, 2, up, 3)
-    w_recv(2)
-    w_send(2, 3, down, 4)
-    transform(2)
-
-    @pl.when(first)
-    def _():
-        for p in (0, 1):
-            e_recv(5, p)
-            if p == 0:
-                e_send(5, p, 6, up, 7)
-            e_recv(6, p)
-            if p == 1:
-                e_send(6, p, 6, down, 7)
-
     w_recv(3)
     w_send(3, 4, up, 5)
     w_recv(4)
@@ -293,21 +296,25 @@
 
     @pl.when(first)
     def _():
-        pltpu.make_async_copy(waves.at[:, 0], eg.at[z, 0], sem_loc.at[5]).wait()
-        for p in (0, 1):
-            e_recv(7, p)
-        for p, (_, z_t, p_t) in enumerate(spots_x()):
+        landed(vg.at[0], vr.at[0])
+        landed(vg.at[2], vr.at[1])
+        for p, (_, _, b, _) in enumerate(spots_x()):
             for ri in (0, 1):
                 for pt in (0, 1):
-                    xa[pt, p, ri] = eg[z_t, p_t, ri, pt]
+                    xa[pt, p, ri] = vg[b, p, ri, pt]
         send(lambda: xa.at[1], lambda: xb.at[1, 0], lambda: x2s.at[1], lambda: x2r.at[1], next_near, 0)
         send(lambda: xa.at[1], lambda: xb.at[1, 1], lambda: x2s.at[2], lambda: x2r.at[2], next_far, 0)
         send(lambda: xa.at[0], lambda: xb.at[0, 0], lambda: x2s.at[0], lambda: x2r.at[0], over, 0)
 
+    k_last = jnp.where(c == 0, (z + 5) % 8, (z + 3) % 8)
+    w_spread(3)
+    w_spread(4)
+    transform(2)
     w_recv(5)
     w_recv(6)
-    k_last = jnp.where(c == 0, (z + 5) % 8, (z + 3) % 8)
-    send(lambda: w.at[:, k_last, e], lambda: w.at[:, k_last, e], lambda: zs.at[6], lambda: zr.at[7], last)
+    hand(w.at[xl, k_last, e], zs.at[6], zr.at[7], last)
+    s_relay(1)
+    s_relay(2)
 
     zero = lax.broadcasted_iota(jnp.int32, (8, 1024), 0) * 0
 
@@ -316,7 +323,7 @@
         landed(xb.at[0, 0], x2r.at[0])
         landed(xb.at[1, 0], x2r.at[1])
         landed(xb.at[1, 1], x2r.at[2])
-        for p, (h_t, _, _) in enumerate(spots_x()):
+        for p, (h_t, _, _, _) in enumerate(spots_x()):
             near = zero + h_t == h
             for ri in (0, 1):
                 tb[p, ri, 1] = jnp.where(near, xa[0, p, ri].astype(F32), xb[0, 0, p, ri].astype(F32)).astype(BF)
@@ -344,8 +351,15 @@
         pair(1, q, left(hre, 0), left(him, 0), trv, tiv)
         pair(3, q, left(tre, 0), left(tim, 0), trc, tic)
 
-    transform(0)
-    transform(1)
+
+    def transform_ab(p):
+        for g in (0, 1):
+            o = dot(lhs[p, g * 128 : g * 128 + 128], tab[...])
+            cols = slice(512, 1024) if g == 0 else slice(0, 512)
+            for t in (0, 1):
+                re, im = o[t * 64 : t * 64 + 32], o[t * 64 + 32 : t * 64 + 64]
+                dens[t, p * 32 : p * 32 + 32, cols] = (re[:, :512] + im[:, 512:]).astype(BF)
+                dens[t, 64 + p * 32 : 96 + p * 32, cols] = (im[:, :512] - re[:, 512:]).astype(BF)
 
     def permute(q):
         p, pt = q // 2, q % 2
@@ -374,13 +388,22 @@
         send(lambda: bl.at[0, :, at], lambda: blp.at[0, :, at], lambda: bs.at[p, 0], lambda: br.at[p, 0], cross)
         send(lambda: ap.at[1 - h, :, at], lambda: app.at[:, at], lambda: bs.at[p, 1], lambda: br.at[p, 1], cross)
 
+    w_spread(5)
+    w_spread(6)
+    transform_ab(0)
     permute(0)
     permute(1)
     share(0)
     w_recv(7)
+    w_spread(7)
+    s_relay(3)
+    s_relay(4)
+    transform_ab(1)
     permute(2)
     permute(3)
     share(1)
+    s_relay(5)
+    s_relay(6)
 
     row_q = lax.broadcasted_iota(jnp.int32, (64, 128), 0) // 16
     lane = lax.broadcasted_iota(jnp.int32, (64, 128), 1)
@@ -396,9 +419,12 @@
     get_cl.wait()
     zb[...] = (dens[3].astype(F32) * cl[...]).astype(BF)
     res[1] = fold(dot_nt(dens[2], zb[...]))
-
+    send(lambda: res.at[1], lambda: part.at[0, 1], lambda: ps.at[3], lambda: pr.at[3], sib)
+
+    s_relay(7)
     for k in range(1, 8):
-        landed(block(k, 1 - e), yr.at[k])
+        landed(block(k, 1 - e, xl), yr.at[k, 0])
+        landed(block(k, 1 - e, 1 - xl), yr.at[k, 1])
 
     def product(b, a):
         wr = w[0].reshape(512, 1024)
@@ -407,24 +433,46 @@
         return fold(dot(a.reshape(128, 512), yb[...]))
 
     res[0] = product(bl, ap[h])
+    send(lambda: res.at[0], lambda: part.at[0, 0], lambda: ps.at[0], lambda: pr.at[0], sib)
     for p in (0, 1):
         at = pl.ds(p * 32, 32)
         landed(blp.at[0, :, at], br.at[p, 0])
         landed(app.at[:, at], br.at[p, 1])
     blp[1, 0] = -blp[0, 1]
     blp[1, 1] = blp[0, 0]
-    send(lambda: res, lambda: part.at[0], lambda: ps.at[0], lambda: pr.at[0], sib)
-    res_far = product(blp, app[...])
-    part[3, 0] = res_far
+    part[3, 0] = product(blp, app[...])
     send(lambda: part.at[3, 0], lambda: part.at[1, 0], lambda: ps.at[1], lambda: pr.at[1], cross)
     send(lambda: part.at[3, 0], lambda: part.at[2, 0], lambda: ps.at[2], lambda: pr.at[2], diag)
-    landed(part.at[0], pr.at[0])
+
+    spot = lax.broadcasted_iota(jnp.int32, (128, 1024), 0)
+    wide = lax.broadcasted_iota(jnp.int32, (128, 1024), 1)
+    lane_l = wide % 256
+    base = (wide // 512) * 64 + c * 32 + ((wide // 256) % 2) * 16
+    row_l = lax.broadcasted_iota(jnp.int32, (16, 1024), 0)
+    wide_l = lax.broadcasted_iota(jnp.int32, (16, 1024), 1) % 256
+
+    def lay(kind, mine, other, col, row):
+        both = jnp.concatenate([mine, other], 0)
+        pick = jnp.where(spot == base + col, F32(1.0), F32(0.0))
+        o = lax.dot_general(
+            both, pick, (((1,), (0,)), ((), ())),
+            precision=lax.Precision.HIGHEST, preferred_element_type=F32,
+        )
+        hit = row_l == row
+        for i, j in ((0, c), (1, 1 - c)):
+            flat = jnp.sum(jnp.where(hit, o[i * 16 : i * 16 + 16], F32(0.0)), 0, keepdims=True)
+            for n in range(4):
+                out[kind, j, n // 2, 0, n % 2 : n % 2 + 1] = flat[:, n * 256 : n * 256 + 256]
+
+    landed(part.at[0, 1], pr.at[3])
+    lay(1, res[1], part[0, 1], lane_l % 16, wide_l // 16)
+    landed(part.at[0, 0], pr.at[0])
     landed(part.at[1, 0], pr.at[1])
     landed(part.at[2, 0], pr.at[2])
-    out[c, 0] = res[0] + part[1, 0]
-    out[c, 1] = res[1]
-    out[1 - c, 0] = part[0, 0] + part[2, 0]
-    out[1 - c, 1] = part[0, 1]
+    lay(
+        0, res[0] + part[1, 0], part[0, 0] + part[2, 0],
+        (lane_l // 64) * 4 + (lane_l // 4) % 4, ((wide_l // 16) % 4) * 4 + wide_l % 4,
+    )
     for make in ends[None]:
         make().wait_send()
 
@@ -445,7 +493,7 @@
     dma = pltpu.SemaphoreType.DMA
     out = pl.pallas_call(
         kernel,
-        out_shape=jax.ShapeDtypeStruct((2, 2, 16, 128), F32),
+        out_shape=jax.ShapeDtypeStruct((2, 2, 2, 1, 2, 256), F32),
         in_specs=[hbm] * 6,
         out_specs=vmem,
         scratch_shapes=[
@@ -466,25 +514,21 @@
             pltpu.VMEM((1024, 1024), BF),
             pltpu.VMEM((2, 4, 1024), jnp.int32),
             pltpu.VMEM((1024,), F32),
-            pltpu.VMEM((8, 2, 2, 2, 8, 1024), BF),
+            pltpu.VMEM((3, 2, 2, 2, 8, 1024), BF),
+            pltpu.VMEM((3, 2, 2, 2, 8, 1024), BF),
             pltpu.VMEM((4, 2, 2, 2, 8, 1024), BF),
             pltpu.VMEM((2, 2, 2, 8, 1024), BF),
             pltpu.VMEM((2, 2, 2, 2, 8, 1024), BF),
             pltpu.SMEM((2, 2), jnp.int32),
-            dma((7,)), dma((7,)), dma((8,)), dma((8,)), dma((8,)), dma((4,)), dma((4,)),
-            dma((7, 2)), dma((8, 2)), dma((1,)), dma((1,)), dma((3, 2)), dma((4, 2)), dma((1,)), dma((2,)),
-            dma((3,)), dma((3,)), dma((2, 2)), dma((2, 2)), dma((3,)), dma((3,)),
+            dma((7,)), dma((7,)), dma((8,)), dma((8,)), dma((8,)), dma((8, 2)), dma((8, 2)), dma((4,)), dma((4,)),
+            dma((3,)), dma((3, 2)), dma((2,)), dma((2,)), dma((3, 2)), dma((4, 2)), dma((1,)), dma((2,)),
+            dma((3,)), dma((3,)), dma((2, 2)), dma((2, 2)), dma((4,)), dma((4,)),
         ],
         compiler_params=pltpu.CompilerParams(
             collective_id=0, has_side_effects=True, vmem_limit_bytes=60 * 1024 * 1024
         ),
     )(transfers, waves, screened, gmap, coulomb, table())
-    r = out.reshape(2, 2, 16, 2, 2, 2, 16)
-    first = lax.axis_index("kx") % 2 == 0
-    r = jnp.where(first, r[:, :, :, :, 0], r[:, :, :, :, 1])
-    direct = r[:, 0].reshape(2, 4, 4, 2, 2, 4, 4).transpose(0, 3, 4, 5, 1, 6, 2)
-    exch = r[:, 1].transpose(0, 2, 3, 1, 4)
-    return direct.reshape(2, 2, 1, 2, 256), exch.reshape(2, 2, 1, 2, 256)
+    return out[0], out[1]
 
 
 def solution(mesh):

time: 53.7 us -> 49.8 us (0.927)
  local copies, waits for them, and re-layouts: 3.78 us -> 1.32 us
  Pallas kernels: 49 us -> 47.7 us
    reshape x3 -> x0, local copies, waits for them, and re-layouts: 2.69 us -> none  [the longest x2 1.56 us: local(): return (direct.reshape(2, 2, 1, 2, 256), exch.reshape(2, 2, 1, 2, 256))]
    pallas_call x1, Pallas kernels: 49 us -> 47.7 us  [local(): pl.pallas_call(kernel, out_shape=jax.ShapeDtypeStruct((2, 2, 2, 1, 2, 256...]
    unnamed x0 -> x1, local copies, waits for them, and re-layouts: none -> 1.32 us
    another operation x2 -> x0, local copies, waits for them, and re-layouts: 1.07 us -> none  [local(): direct = r[:, 0].reshape(2, 4, 4, 2, 2, 4, 4).transpose(0, 3, 4, 5, 1, 6, 2)]
where the time goes in v2:
time: 49.8 us; the launch traced here: 49.6 us
  Pallas kernels  47.7 us (96%)
  local copies, waits for them, and re-layouts  1.32 us (3%)
  between operations  0.64 us (1%)
    pallas_call x1, Pallas kernels, local(): pl.pallas_call(kernel, out_shape=jax.ShapeDtypeStruct((2, 2, 2, 1, 2, 256...  47.7 us
    unnamed x1, local copies, waits for them, and re-layouts  1.32 us

profile of v2, /device:TPU:1, one launch (start us, length us, event | category | flops | bytes accessed | tf_op | source)
XLA Modules:
  0.0 49.6 jit_solution(2005018416703909849)
XLA Ops:
  0.6 47.7 %shard_map.77 = f32[2,2,2,1,2,256]{5,4,3,2,1,0:T(2,128)} custom-call(s32[2,2]{1,0:T(2,128)} %transfers.1, bf16[2,1,2,8,1024]{4,3,2,1,0:T(8,128)(2,1)} %waves.1, bf16[2,2,32,1024]{3,2,1,0:T(8,128)(2,1)} %scr.1, s32[2,4,1024]{2,1,0:T(4,128)} %gmap.1, f32[1024]{0:T(1024)} %coulomb.1, bf16[1024,1024]{1,0:T(8,128)(2,1)} %constant.2.clone.tab_hbm), custom_call_target="tpu_custom_call" | custom-call | tf_op jit(solution)/shard_map/pallas_call | solution.py:494
  48.3 1.3 %slice_bitcast_fusion = (f32[2,2,1,2,256]{4,3,2,1,0:T(2,128)}, f32[2,2,1,2,256]{4,3,2,1,0:T(2,128)}) fusion(f32[2,2,2,1,2,256]{5,4,3,2,1,0:T(2,128)} %shard_map.77), kind=kLoop, calls=%fused_computation | loop fusion | bytes 32768

commit v3 on v2

--- a/solution.py
+++ b/solution.py
@@ -33,7 +33,7 @@
 
 def kernel(
     transfers, waves, scr, gmap, coulomb, tab_hbm, out,
-    w, hb, tb, lhs, dens, hot, bl, ap, blp, app, yb, zb, res, part,
+    w, hb, tb, lhs, dens, hot, bl, ap, hbf, tbf, yb, zb, res, part,
     tab, gm, cl, eg, vg, fg, xa, xb, tr,
     sem_loc, zs, zr, qs, qr, ys, yr, ss, sr,
     es, er, vs, vr, fs, fr, fas, far, x2s, x2r, bs, br, ps, pr,
@@ -152,6 +152,8 @@
         send(lambda: waves.at[:, 0], lambda: eg.at[1, 1], lambda: es.at[2], lambda: er.at[1, 1], sib, 1)
 
     send(lambda: scr.at[1 - c], lambda: w.at[:, z, c], lambda: ss.at[2], lambda: sr.at[2], sib)
+    send(lambda: waves.at[:, 0], lambda: hbf.at[c], lambda: bs.at[0], lambda: br.at[c], cross)
+    send(lambda: waves.at[:, 0], lambda: hbf.at[c], lambda: bs.at[1], lambda: br.at[c], diag)
     send(lambda: waves.at[:, 0], lambda: hb.at[c], lambda: ss.at[0], lambda: sr.at[0], sib)
 
     @pl.when(second)
@@ -256,6 +258,20 @@
             got.append((((m * 2 + step) % 32) // 16, a + 1, b + 1, step % 2))
         return got
 
+    def build(q, far):
+        p, pt = q // 2, q % 2
+        m_q = (m + 8) % 16 if far else m
+        ky_q = other_ky if far else ky
+        wx = jnp.where(m_q * 2 + p + tr[c, 0] >= 32, 1, 0)
+        wy = jnp.where(ky_q * 2 + pt + tr[c, 1] >= 16, 2, 0)
+        row = gm[c, pl.ds(wx + wy, 1), :]
+        hot[far * 4 + q] = jnp.where(
+            lax.broadcasted_iota(jnp.int32, (1024, 1024), 0) == row, F32(1.0), F32(0.0)
+        ).astype(BF)
+
+    for q in range(4):
+        build(q, 0)
+        build(q, 1)
     w_recv(1)
     w_send(1, 2, up, 3)
     w_recv(2)
@@ -313,6 +329,8 @@
     w_recv(5)
     w_recv(6)
     hand(w.at[xl, k_last, e], zs.at[6], zr.at[7], last)
+    w_spread(5)
+    w_spread(6)
     s_relay(1)
     s_relay(2)
 
@@ -340,17 +358,22 @@
                         near, fg[y_t, p, ri, p_t].astype(F32), xb[0, pt, p, ri].astype(F32)
                     ).astype(BF)
 
-    for q in range(4):
-        p, pt = q // 2, q % 2
-        hre = hb[p, 0, pt].astype(F32)
-        him = hb[p, 1, pt].astype(F32)
-        tre = tb[p, 0, pt].astype(F32)
-        tim = tb[p, 1, pt].astype(F32)
-        (trv, trc), (tiv, tic) = right(tre), right(tim)
-        pair(0, q, left(hre, 4), left(him, 4), trc, tic)
-        pair(1, q, left(hre, 0), left(him, 0), trv, tiv)
-        pair(3, q, left(tre, 0), left(tim, 0), trc, tic)
-
+    send(lambda: tb, lambda: tbf, lambda: bs.at[2], lambda: br.at[2], cross)
+
+    def pairs_ab(left_waves, right_waves, with_x):
+        for q in range(4):
+            p, pt = q // 2, q % 2
+            hre = left_waves[p, 0, pt].astype(F32)
+            him = left_waves[p, 1, pt].astype(F32)
+            tre = right_waves[p, 0, pt].astype(F32)
+            tim = right_waves[p, 1, pt].astype(F32)
+            (trv, trc), (tiv, tic) = right(tre), right(tim)
+            pair(0, q, left(hre, 4), left(him, 4), trc, tic)
+            pair(1, q, left(hre, 0), left(him, 0), trv, tiv)
+            if with_x:
+                pair(3, q, left(tre, 0), left(tim, 0), trc, tic)
+
+    pairs_ab(hb, tb, True)
 
     def transform_ab(p):
         for g in (0, 1):
@@ -361,50 +384,33 @@
                 dens[t, p * 32 : p * 32 + 32, cols] = (re[:, :512] + im[:, 512:]).astype(BF)
                 dens[t, 64 + p * 32 : 96 + p * 32, cols] = (im[:, :512] - re[:, 512:]).astype(BF)
 
-    def permute(q):
-        p, pt = q // 2, q % 2
-        wx = jnp.where(m * 2 + p + tr[c, 0] >= 32, 1, 0)
-        wy = jnp.where(ky * 2 + pt + tr[c, 1] >= 16, 2, 0)
-        row = gm[c, pl.ds(wx + wy, 1), :]
-        hot[...] = jnp.where(
-            lax.broadcasted_iota(jnp.int32, (1024, 1024), 0) == row, F32(1.0), F32(0.0)
-        ).astype(BF)
+    def permute(q, far):
         at = slice(q * 16, q * 16 + 16)
         rows = jnp.concatenate(
             [dens[0, at], dens[0, 64 + q * 16 : 80 + q * 16], dens[1, at], dens[1, 64 + q * 16 : 80 + q * 16]], 0
         )
-        o = dot(rows, hot[...]).astype(BF)
+        o = dot(rows, hot[far * 4 + q]).astype(BF)
         for hh in (0, 1):
             cols = slice(hh * 512, hh * 512 + 512)
-            ap[hh, 0, at] = o[0:16, cols]
-            ap[hh, 1, at] = o[16:32, cols]
-        bl[0, 0, at] = o[32:48]
-        bl[0, 1, at] = o[48:64]
-        bl[1, 0, at] = -o[48:64]
-        bl[1, 1, at] = o[32:48]
-
-    def share(p):
-        at = pl.ds(p * 32, 32)
-        send(lambda: bl.at[0, :, at], lambda: blp.at[0, :, at], lambda: bs.at[p, 0], lambda: br.at[p, 0], cross)
-        send(lambda: ap.at[1 - h, :, at], lambda: app.at[:, at], lambda: bs.at[p, 1], lambda: br.at[p, 1], cross)
-
-    w_spread(5)
-    w_spread(6)
+            ap[far, hh, 0, at] = o[0:16, cols]
+            ap[far, hh, 1, at] = o[16:32, cols]
+        bl[0, far, 0, at] = o[32:48]
+        bl[0, far, 1, at] = o[48:64]
+        bl[1, far, 0, at] = -o[48:64]
+        bl[1, far, 1, at] = o[32:48]
+
     transform_ab(0)
-    permute(0)
-    permute(1)
-    share(0)
     w_recv(7)
     w_spread(7)
     s_relay(3)
+    permute(0, 0)
     s_relay(4)
+    permute(1, 0)
     transform_ab(1)
-    permute(2)
-    permute(3)
-    share(1)
     s_relay(5)
+    permute(2, 0)
+    permute(3, 0)
     s_relay(6)
-
     row_q = lax.broadcasted_iota(jnp.int32, (64, 128), 0) // 16
     lane = lax.broadcasted_iota(jnp.int32, (64, 128), 1)
     keep = row_q == (lane % 64) // 16
@@ -421,26 +427,28 @@
     res[1] = fold(dot_nt(dens[2], zb[...]))
     send(lambda: res.at[1], lambda: part.at[0, 1], lambda: ps.at[3], lambda: pr.at[3], sib)
 
+
+    landed(hbf.at[0], br.at[0])
+    landed(hbf.at[1], br.at[1])
+    landed(tbf, br.at[2])
+    pairs_ab(hbf, tbf, False)
+    transform_ab(0)
     s_relay(7)
+    permute(0, 1)
+    permute(1, 1)
+    transform_ab(1)
+    permute(2, 1)
+    permute(3, 1)
+
     for k in range(1, 8):
         landed(block(k, 1 - e, xl), yr.at[k, 0])
         landed(block(k, 1 - e, 1 - xl), yr.at[k, 1])
-
-    def product(b, a):
-        wr = w[0].reshape(512, 1024)
-        wi = w[1].reshape(512, 1024)
-        yb[...] = (dot_nt(wr, b[0].reshape(128, 1024)) + dot_nt(wi, b[1].reshape(128, 1024))).astype(BF)
-        return fold(dot(a.reshape(128, 512), yb[...]))
-
-    res[0] = product(bl, ap[h])
+    wr = w[0].reshape(512, 1024)
+    wi = w[1].reshape(512, 1024)
+    yb[...] = (dot_nt(wr, bl[0].reshape(256, 1024)) + dot_nt(wi, bl[1].reshape(256, 1024))).astype(BF)
+    part[3, 0] = fold(dot(ap[1, h].reshape(128, 512), yb[:, 128:]))
+    res[0] = fold(dot(ap[0, h].reshape(128, 512), yb[:, :128]))
     send(lambda: res.at[0], lambda: part.at[0, 0], lambda: ps.at[0], lambda: pr.at[0], sib)
-    for p in (0, 1):
-        at = pl.ds(p * 32, 32)
-        landed(blp.at[0, :, at], br.at[p, 0])
-        landed(app.at[:, at], br.at[p, 1])
-    blp[1, 0] = -blp[0, 1]
-    blp[1, 1] = blp[0, 0]
-    part[3, 0] = product(blp, app[...])
     send(lambda: part.at[3, 0], lambda: part.at[1, 0], lambda: ps.at[1], lambda: pr.at[1], cross)
     send(lambda: part.at[3, 0], lambda: part.at[2, 0], lambda: ps.at[2], lambda: pr.at[2], diag)
 
@@ -502,12 +510,12 @@
             pltpu.VMEM((2, 2, 2, 8, 1024), BF),
             pltpu.VMEM((4, 256, 1024), BF),
             pltpu.VMEM((4, 128, 1024), BF),
-            pltpu.VMEM((1024, 1024), BF),
-            pltpu.VMEM((2, 2, 64, 1024), BF),
-            pltpu.VMEM((2, 2, 64, 512), BF),
-            pltpu.VMEM((2, 2, 64, 1024), BF),
-            pltpu.VMEM((2, 64, 512), BF),
-            pltpu.VMEM((512, 128), BF),
+            pltpu.VMEM((8, 1024, 1024), BF),
+            pltpu.VMEM((2, 2, 2, 64, 1024), BF),
+            pltpu.VMEM((2, 2, 2, 64, 512), BF),
+            pltpu.VMEM((2, 2, 2, 8, 1024), BF),
+            pltpu.VMEM((2, 2, 2, 8, 1024), BF),
+            pltpu.VMEM((512, 256), BF),
             pltpu.VMEM((128, 1024), BF),
             pltpu.VMEM((2, 16, 128), F32),
             pltpu.VMEM((4, 2, 16, 128), F32),
@@ -522,7 +530,7 @@
             pltpu.SMEM((2, 2), jnp.int32),
             dma((7,)), dma((7,)), dma((8,)), dma((8,)), dma((8,)), dma((8, 2)), dma((8, 2)), dma((4,)), dma((4,)),
             dma((3,)), dma((3, 2)), dma((2,)), dma((2,)), dma((3, 2)), dma((4, 2)), dma((1,)), dma((2,)),
-            dma((3,)), dma((3,)), dma((2, 2)), dma((2, 2)), dma((4,)), dma((4,)),
+            dma((3,)), dma((3,)), dma((3,)), dma((3,)), dma((4,)), dma((4,)),
         ],
         compiler_params=pltpu.CompilerParams(
             collective_id=0, has_side_effects=True, vmem_limit_bytes=60 * 1024 * 1024

time: 49.8 us -> 48.8 us (0.980)
  Pallas kernels: 47.7 us -> 46.7 us
    pallas_call x1, Pallas kernels: 47.7 us -> 46.7 us  [local(): pl.pallas_call(kernel, out_shape=jax.ShapeDtypeStruct((2, 2, 2, 1, 2, 256...]
where the time goes in v3:
time: 48.8 us; the launch traced here: 48.7 us
  Pallas kernels  46.7 us (96%)
  local copies, waits for them, and re-layouts  1.32 us (3%)
  between operations  0.64 us (1%)
    pallas_call x1, Pallas kernels, local(): pl.pallas_call(kernel, out_shape=jax.ShapeDtypeStruct((2, 2, 2, 1, 2, 256...  46.7 us
    unnamed x1, local copies, waits for them, and re-layouts  1.32 us

profile of v3, /device:TPU:1, one launch (start us, length us, event | category | flops | bytes accessed | tf_op | source)
XLA Modules:
  0.0 48.7 jit_solution(6864355075983227424)
XLA Ops:
  0.6 46.7 %shard_map.77 = f32[2,2,2,1,2,256]{5,4,3,2,1,0:T(2,128)} custom-call(s32[2,2]{1,0:T(2,128)} %transfers.1, bf16[2,1,2,8,1024]{4,3,2,1,0:T(8,128)(2,1)} %waves.1, bf16[2,2,32,1024]{3,2,1,0:T(8,128)(2,1)} %scr.1, s32[2,4,1024]{2,1,0:T(4,128)} %gmap.1, f32[1024]{0:T(1024)} %coulomb.1, bf16[1024,1024]{1,0:T(8,128)(2,1)} %constant.2.clone.tab_hbm), custom_call_target="tpu_custom_call" | custom-call | tf_op jit(solution)/shard_map/pallas_call | solution.py:502
  47.3 1.3 %slice_bitcast_fusion = (f32[2,2,1,2,256]{4,3,2,1,0:T(2,128)}, f32[2,2,1,2,256]{4,3,2,1,0:T(2,128)}) fusion(f32[2,2,2,1,2,256]{5,4,3,2,1,0:T(2,128)} %shard_map.77), kind=kLoop, calls=%fused_computation | loop fusion | bytes 32768

commit v4 on v3

--- a/solution.py
+++ b/solution.py
@@ -474,6 +474,19 @@
 
     landed(part.at[0, 1], pr.at[3])
     lay(1, res[1], part[0, 1], lane_l % 16, wide_l // 16)
+    for make in ends[None]:
+        make().wait_send()
+
+    @pl.when(first)
+    def _():
+        for make in ends[0]:
+            make().wait_send()
+
+    @pl.when(second)
+    def _():
+        for make in ends[1]:
+            make().wait_send()
+
     landed(part.at[0, 0], pr.at[0])
     landed(part.at[1, 0], pr.at[1])
     landed(part.at[2, 0], pr.at[2])
@@ -481,18 +494,6 @@
         0, res[0] + part[1, 0], part[0, 0] + part[2, 0],
         (lane_l // 64) * 4 + (lane_l // 4) % 4, ((wide_l // 16) % 4) * 4 + wide_l % 4,
     )
-    for make in ends[None]:
-        make().wait_send()
-
-    @pl.when(first)
-    def _():
-        for make in ends[0]:
-            make().wait_send()
-
-    @pl.when(second)
-    def _():
-        for make in ends[1]:
-            make().wait_send()
 
 
 def local(waves, screened, coulomb, transfers, gmap):

time: 48.8 us -> 48.7 us (level)
  no operation moved by 1% of the time
where the time goes in v4:
time: 48.7 us; the launch traced here: 48.6 us
  Pallas kernels  46.6 us (96%)
  local copies, waits for them, and re-layouts  1.32 us (3%)
  between operations  0.64 us (1%)
    pallas_call x1, Pallas kernels, local(): pl.pallas_call(kernel, out_shape=jax.ShapeDtypeStruct((2, 2, 2, 1, 2, 256...  46.6 us
    unnamed x1, local copies, waits for them, and re-layouts  1.32 us

profile of v4, /device:TPU:1, one launch (start us, length us, event | category | flops | bytes accessed | tf_op | source)
XLA Modules:
  0.0 48.6 jit_solution(1568764004817818567)
XLA Ops:
  0.6 46.6 %shard_map.77 = f32[2,2,2,1,2,256]{5,4,3,2,1,0:T(2,128)} custom-call(s32[2,2]{1,0:T(2,128)} %transfers.1, bf16[2,1,2,8,1024]{4,3,2,1,0:T(8,128)(2,1)} %waves.1, bf16[2,2,32,1024]{3,2,1,0:T(8,128)(2,1)} %scr.1, s32[2,4,1024]{2,1,0:T(4,128)} %gmap.1, f32[1024]{0:T(1024)} %coulomb.1, bf16[1024,1024]{1,0:T(8,128)(2,1)} %constant.2.clone.tab_hbm), custom_call_target="tpu_custom_call" | custom-call | tf_op jit(solution)/shard_map/pallas_call | solution.py:503
  47.3 1.3 %slice_bitcast_fusion = (f32[2,2,1,2,256]{4,3,2,1,0:T(2,128)}, f32[2,2,1,2,256]{4,3,2,1,0:T(2,128)}) fusion(f32[2,2,2,1,2,256]{5,4,3,2,1,0:T(2,128)} %shard_map.77), kind=kLoop, calls=%fused_computation | loop fusion | bytes 32768
